TPU v7x, 256 devices: a whole 4x4x8 slice. The times are simulated.
256 devices in a mesh: grp: 32 (over x, y, core), tp: 8 (over z).
Axes of the slice: x: 4, y: 4, z: 8, core: 2. Of those that a mesh axis runs over, the one named last changes fastest.
Arguments:
- hidden_in: bfloat16 [512, 2048], P('grp'), may hold values from -6 to 6
- norm_gain: bfloat16 [2048], replicated, may hold values from 0.099609375 to 1.8984375
- w_query: bfloat16 [2048, 2048], P(None, 'tp'), may hold values from -0.125 to 0.125
- w_keyval: bfloat16 [2048, 512], P(None, 'tp'), may hold values from -0.125 to 0.125
- w_output: bfloat16 [2048, 2048], P('tp'), may hold values from -0.125 to 0.125
- prefix_cache: bfloat16 [64, 512, 512], P('grp', 'tp'), may hold values from -130 to 130
- private_cache: bfloat16 [512, 512, 512], P('grp', 'tp'), may hold values from -130 to 130
- node_parent: int32 [64], replicated, may hold values from 0 to 3, as said below
- node_length: int32 [64], replicated, may hold values from 1 to 512, as said below
- request_node: int32 [512], replicated, may hold values from 4 to 63, as said below
- private_length: int32 [512], P('grp'), may hold values from 0 to 512, as said below
Outputs:
- hidden_out: bfloat16 [512, 2048], P('grp', 'tp')
- new_keyval: bfloat16 [512, 512], P('grp', 'tp')
Inputs may be any that keep to these rules, and one draw needn't show every extreme that they name: `node_parent`: nodes 0 to 3 are the tenants' roots and are their own parents; every other node's parent is a root, and every root has a child. `request_node`: request r belongs to tenant r // 128; its node is a non-root node whose parent is that tenant's root. `node_length`: the longest node has exactly 512 used slots. `private_length`: some request has exactly 512 used slots.
All inputs are finite; a program needn't handle non-finite values.
Results may differ from a plain program's by a relative error of at most 0.023.
Values may be sent and summed in bfloat16 or wider, within the bound.
A program may use at most 128 MiB of HBM per device.

v0:
```python
import math
import jax
import jax.numpy as jnp
from jax import lax
from jax.sharding import PartitionSpec as P

HEADS = 32
KV_HEADS = 4
HEAD_DIM = 64
TENANTS = 4


def combined_all(x, axis, combine):
    everything = jax.tree.map(
        lambda part, kind: lax.all_gather(part.astype(kind), axis),
        x,
        (jnp.bfloat16, jnp.bfloat16, jnp.bfloat16),
    )

    def take(k):
        return jax.tree.map(lambda part, own: part[k].astype(own.dtype), everything, x)

    return lax.fori_loop(
        1, lax.axis_size(axis), lambda k, so_far: combine(so_far, take(k)), take(0)
    )


def rms_norm(values, scale_gain):
    floats = values.astype(jnp.float32)
    spread = jnp.mean(floats * floats, axis=-1, keepdims=True)
    return (floats * lax.rsqrt(spread + 1e-05) * scale_gain.astype(jnp.float32)).astype(
        jnp.bfloat16
    )


def rotate(head_rows, position):
    half_dim = head_rows.shape[-1] // 2
    freq_index = jnp.arange(half_dim, dtype=jnp.float32)
    frequency = jnp.exp(freq_index * (-2.0 * math.log(10000.0) / head_rows.shape[-1]))
    angles = position[:, None, None] * frequency[None, None, :]
    cosine = jnp.cos(angles)
    sine_part = jnp.sin(angles)
    front_half = head_rows[..., :half_dim]
    back_half = head_rows[..., half_dim:]
    return jnp.concatenate(
        [front_half * cosine - back_half * sine_part, back_half * cosine + front_half * sine_part],
        axis=-1,
    )


def softmax_part(queries, key_rows, value_rows, valid, shared):
    row_count = queries.shape[0]
    grouped = queries.reshape(row_count, KV_HEADS, HEADS // KV_HEADS, HEAD_DIM)
    if shared:
        scores = jnp.einsum("nkgd,lkd->nkgl", grouped, key_rows, preferred_element_type=jnp.float32)
    else:
        scores = jnp.einsum(
            "nkgd,nlkd->nkgl", grouped, key_rows, preferred_element_type=jnp.float32
        )
    scores = scores * HEAD_DIM ** (-0.5)
    usable = valid[:, None, None, :]
    scores = jnp.where(usable, scores, -jnp.inf)
    maxima = jnp.maximum(jnp.max(scores, axis=-1), -1e30)
    weights = jnp.where(usable, jnp.exp(scores - maxima[..., None]), 0.0)
    totals = jnp.sum(weights, axis=-1)
    rounded = weights.astype(jnp.bfloat16)
    if shared:
        weighted = jnp.einsum(
            "nkgl,lkd->nkgd", rounded, value_rows, preferred_element_type=jnp.float32
        )
    else:
        weighted = jnp.einsum(
            "nkgl,nlkd->nkgd", rounded, value_rows, preferred_element_type=jnp.float32
        )
    return (weighted, maxima, totals)


def merge_pair(left_part, right_part):
    left_sum, left_max, left_total = left_part
    right_sum, right_max, right_total = right_part
    upper = jnp.maximum(left_max, right_max)
    left_factor = jnp.exp(left_max - upper)
    right_factor = jnp.exp(right_max - upper)
    merged_sum = left_sum * left_factor[..., None] + right_sum * right_factor[..., None]
    return (merged_sum, upper, left_total * left_factor + right_total * right_factor)


def add_token(weighted, maxima, totals, token_score, token_value, form):
    upper = jnp.maximum(maxima, token_score)
    former = jnp.exp(maxima - upper)
    fresh = jnp.exp(token_score - upper)
    summed = weighted * former[..., None] + jnp.einsum(
        form, fresh.astype(jnp.bfloat16), token_value, preferred_element_type=jnp.float32
    )
    return summed / (totals * former + fresh)[..., None]


def on_device(
    hidden_in,
    norm_gain,
    w_query,
    w_keyval,
    w_output,
    prefix_cache,
    private_cache,
    node_parent,
    node_length,
    request_node,
    private_length,
):
    grp_index = lax.axis_index("grp")
    tp_index = lax.axis_index("tp")
    req_dev = hidden_in.shape[0]
    total_req = request_node.shape[0]
    per_tenant = total_req // TENANTS
    share_count = HEADS // KV_HEADS
    key_width = KV_HEADS * HEAD_DIM
    local_heads = w_query.shape[1] // HEAD_DIM
    local_kv = w_keyval.shape[1] // HEAD_DIM
    slice_width = local_heads * HEAD_DIM
    node_dev = prefix_cache.shape[0]
    local_len = prefix_cache.shape[1]
    priv_len = private_cache.shape[1]
    scale_factor = HEAD_DIM ** (-0.5)
    normed = rms_norm(hidden_in, norm_gain)
    query = jnp.dot(normed, w_query, preferred_element_type=jnp.float32)
    keyval = jnp.dot(normed, w_keyval, preferred_element_type=jnp.float32)
    own_mid = lax.dynamic_slice_in_dim(request_node, grp_index * req_dev, req_dev)
    own_root = node_parent[own_mid]
    position = (node_length[own_root] + node_length[own_mid] + private_length).astype(jnp.float32)
    query_rot = (
        rotate(query.reshape(req_dev, local_heads, HEAD_DIM), position)
        .reshape(req_dev, slice_width)
        .astype(jnp.bfloat16)
    )
    kv_rows = keyval.reshape(req_dev, local_kv, HEAD_DIM)
    is_key = tp_index * local_kv + jnp.arange(local_kv) < KV_HEADS
    new_keyval = (
        jnp.where(is_key[None, :, None], rotate(kv_rows, position), kv_rows)
        .reshape(req_dev, local_kv * HEAD_DIM)
        .astype(jnp.bfloat16)
    )
    query_all, keyval_all = (
        lax.all_gather(query_rot, "tp", axis=1, tiled=True),
        lax.all_gather(new_keyval, "tp", axis=1, tiled=True),
    )
    everyone = lax.all_gather(query_all, "grp", axis=0, tiled=True)
    private_valid = (tp_index * priv_len + jnp.arange(priv_len))[None, :] < private_length[:, None]
    private_keys = private_cache[:, :, :key_width].reshape(req_dev, priv_len, KV_HEADS, HEAD_DIM)
    private_values = private_cache[:, :, key_width:].reshape(req_dev, priv_len, KV_HEADS, HEAD_DIM)
    private_part = softmax_part(query_all, private_keys, private_values, private_valid, False)
    slot_positions = tp_index * local_len + jnp.arange(local_len)
    node_parts = []
    for node_slot in range(node_dev):
        node_id = grp_index * node_dev + node_slot
        is_root = node_id < TENANTS
        member = jnp.where(is_root, node_parent[request_node] == node_id, request_node == node_id)
        order_key = jnp.where(member, 0, total_req) + jnp.arange(total_req)
        picked = lax.top_k(-order_key, per_tenant)[1]
        filled = jnp.arange(per_tenant) < jnp.sum(member.astype(jnp.int32))
        chosen = jnp.take(everyone, picked, axis=0)
        node_rows = prefix_cache[node_slot]
        node_keys = node_rows[:, :key_width].reshape(local_len, KV_HEADS, HEAD_DIM)
        node_values = node_rows[:, key_width:].reshape(local_len, KV_HEADS, HEAD_DIM)
        node_valid = (slot_positions < node_length[node_id])[None, :]
        weighted, maxima, totals = softmax_part(chosen, node_keys, node_values, node_valid, True)
        level_slot = jnp.where(is_root, 0, 1)
        node_parts.append((picked, filled, level_slot, weighted, maxima, totals))
    sum_rows = jnp.zeros((total_req, 2, HEADS * HEAD_DIM), jnp.float32)
    max_rows = jnp.zeros((total_req, 2, HEADS), jnp.float32)
    total_rows = jnp.zeros((total_req, 2, HEADS), jnp.float32)
    for entry in node_parts:
        picked, filled, level_slot, weighted, maxima, totals = entry
        keep = filled[:, None]
        sum_rows = sum_rows.at[picked, level_slot].add(
            jnp.where(keep, weighted.reshape(per_tenant, HEADS * HEAD_DIM), 0.0)
        )
        max_rows = max_rows.at[picked, level_slot].add(
            jnp.where(keep, maxima.reshape(per_tenant, HEADS), 0.0)
        )
        total_rows = total_rows.at[picked, level_slot].add(
            jnp.where(keep, totals.reshape(per_tenant, HEADS), 0.0)
        )
    back_sum, back_max, back_total = (
        lax.psum_scatter(sum_rows, "grp", scatter_dimension=0, tiled=True),
        lax.psum_scatter(max_rows, "grp", scatter_dimension=0, tiled=True),
        lax.psum_scatter(total_rows, "grp", scatter_dimension=0, tiled=True),
    )
    stat_shape = (req_dev, 2, KV_HEADS, share_count)
    back_sum = back_sum.reshape(req_dev, 2, KV_HEADS, share_count, HEAD_DIM)
    back_max = back_max.reshape(stat_shape)
    back_total = back_total.reshape(stat_shape)
    root_part = (back_sum[:, 0], back_max[:, 0], back_total[:, 0])
    mid_part = (back_sum[:, 1], back_max[:, 1], back_total[:, 1])
    local_sum, local_max, local_total = merge_pair(merge_pair(root_part, mid_part), private_part)
    full_sum, full_max, full_total = combined_all(
        (local_sum, local_max, local_total), "tp", merge_pair
    )
    grouped = query_all.reshape(req_dev, KV_HEADS, share_count, HEAD_DIM)
    token_keys = keyval_all[:, :key_width].reshape(req_dev, KV_HEADS, HEAD_DIM)
    token_values = keyval_all[:, key_width:].reshape(req_dev, KV_HEADS, HEAD_DIM)
    token_score = (
        jnp.einsum("nkgd,nkd->nkg", grouped, token_keys, preferred_element_type=jnp.float32)
        * scale_factor
    )
    attention_all = (
        add_token(full_sum, full_max, full_total, token_score, token_values, "nkg,nkd->nkgd")
        .reshape(req_dev, HEADS * HEAD_DIM)
        .astype(jnp.bfloat16)
    )
    attention = lax.dynamic_slice_in_dim(attention_all, tp_index * slice_width, slice_width, 1)
    projected = jnp.dot(attention, w_output, preferred_element_type=jnp.float32)
    summed = lax.psum_scatter(
        projected.astype(jnp.bfloat16), "tp", scatter_dimension=1, tiled=True
    ).astype(jnp.float32)
    out_width = summed.shape[1]
    residual = lax.dynamic_slice_in_dim(hidden_in, tp_index * out_width, out_width, 1).astype(
        jnp.float32
    )
    hidden_out = (summed + residual).astype(jnp.bfloat16)
    return (hidden_out, new_keyval)


def solution(mesh):
    placed = (
        P("grp", None),
        P(),
        P(None, "tp"),
        P(None, "tp"),
        P("tp", None),
        P("grp", "tp", None),
        P("grp", "tp", None),
        P(),
        P(),
        P(),
        P("grp"),
    )
    return jax.shard_map(
        on_device,
        mesh=mesh,
        in_specs=placed,
        out_specs=(P("grp", "tp"), P("grp", "tp")),
        check_vma=False,
    )
```

profile of v0, /device:TPU:10, one launch (start us, length us, event | category | flops | bytes accessed | tf_op | source)
XLA Modules:
  0.0 476.1 jit_solution(16032584762213668495)
XLA Ops:
  16.5 30.2 %all_gather.23 = bf16[16,2048]{1,0:T(8,128)(2,1)} all-gather(bf16[16,256]{1,0:T(8,128)(2,1)S(1)} %convert_element_type.140), channel_id=1, replica_groups=mesh['grp'=32,'tp'=8] {'tp'}, dimensions={1}, use_global_device_ids=true | all-gather | bytes 73728 | tf_op jit(solution)/shard_map/all_gather | solution.py:144
  49.7 2.1 fusion.87
  51.8 2.1 fusion.88
  53.8 2.1 fusion.89
  55.9 41.3 %convert_reduce_fusion = (s32[]{:T(128)}, pred[512]{0:T(512)(128)(4,1)S(1)}, s32[512]{0:T(512)S(1)}) fusion(s32[512]{0:T(512)} %param.24, s32[]{:T(128)S(6)} %add.231, pred[]{:T(512)S(6)} %lt.150, s32[]{:T(128)} %bitcast.67, s32[]{:T(128)} %bitcast.66, s32[]{:T(128)} %bitcast.65, s32[]{:T(128)} %bitcast.64, s32[]{:T(128)} %bitcast.63, s32[]{:T(128)} %bitcast.62, ...), kind=kLoop, calls=%fused_computation.153 | loop fusion | flops 68607 | bytes 4873 | tf_op jit(solution)/shard_map/reduce_sum | solution.py:160
  98.6 3.8 top_k.17
  102.3 3.8 top_k.24
  110.2 4.3 gather_fusion.3
  116.4 2.0 copy.74
  129.9 2.1 fusion.16
  134.8 6.8 %scatter_fusion.4 = f32[512,2,32]{2,1,0:T(2,128)S(1)} fusion(f32[512,2,32]{2,1,0:T(2,128)S(1)} %broadcast.255.clone.1, s32[128]{0:T(128)S(1)} %fusion.77, f32[128,32]{1,0:T(8,128)S(1)} %copy.94), kind=kCustom, calls=%fused_computation.9 | custom fusion | flops 4096 | bytes 50176 | tf_op jit(solution)/shard_map/scatter-add | solution.py:181
  141.7 6.6 %scatter_fusion.2 = f32[512,2,32]{2,1,0:T(2,128)S(1)} fusion(f32[512,2,32]{2,1,0:T(2,128)S(1)} %broadcast.255.clone, s32[128]{0:T(128)S(1)} %fusion.77, f32[128,32]{1,0:T(8,128)S(1)} %copy.83), kind=kCustom, calls=%fused_computation.7 | custom fusion | flops 4096 | bytes 50176 | tf_op jit(solution)/shard_map/scatter-add | solution.py:178
  148.3 6.6 %scatter_fusion.5 = f32[512,2,32]{2,1,0:T(2,128)S(1)} fusion(f32[512,2,32]{2,1,0:T(2,128)S(1)} %scatter_fusion.4, s32[128]{0:T(128)S(1)} %fusion.78, f32[128,32]{1,0:T(8,128)S(1)} %copy.95), kind=kCustom, calls=%fused_computation.10 | custom fusion | flops 4096 | bytes 50176 | tf_op jit(solution)/shard_map/scatter-add | solution.py:181
  154.9 6.6 %scatter_fusion.3 = f32[512,2,32]{2,1,0:T(2,128)S(1)} fusion(f32[512,2,32]{2,1,0:T(2,128)S(1)} %scatter_fusion.2, s32[128]{0:T(128)S(1)} %fusion.78, f32[128,32]{1,0:T(8,128)S(1)} %copy.84), kind=kCustom, calls=%fused_computation.8 | custom fusion | flops 4096 | bytes 50176 | tf_op jit(solution)/shard_map/scatter-add | solution.py:178
  161.5 7.5 %broadcast_in_dim.180 = f32[512,2,2048]{2,1,0:T(2,128)} broadcast(f32[]{:T(128)} %constant.85.clone.1), dimensions={} | broadcast | bytes 8388612 | tf_op jit(solution)/shard_map/broadcast_in_dim | solution.py:169
  169.0 21.2 %scatter_fusion = f32[512,2,2048]{2,1,0:T(2,128)} fusion(f32[512,2,2048]{2,1,0:T(2,128)} %broadcast_in_dim.180, s32[128]{0:T(128)S(1)} %fusion.77, f32[128,2048]{1,0:T(8,128)S(1)} %broadcast_select_fusion.1), kind=kCustom, calls=%fused_computation.5 | custom fusion | flops 262144 | bytes 3146752 | tf_op jit(solution)/shard_map/scatter-add | solution.py:175
  190.3 22.7 %scatter_fusion.1 = f32[512,2,2048]{2,1,0:T(2,128)} fusion(f32[512,2,2048]{2,1,0:T(2,128)} %scatter_fusion, s32[128]{0:T(128)S(1)} %fusion.78, f32[128,2048]{1,0:T(8,128)} %broadcast_select_fusion), kind=kCustom, calls=%fused_computation.6 | custom fusion | flops 262144 | bytes 3146752 | tf_op jit(solution)/shard_map/scatter-add | solution.py:175
  218.5 24.5 %all-gather.1 = bf16[8,64,16]{1,2,0:T(8,128)(2,1)S(1)} all-gather(bf16[1,64,16]{1,2,0:T(8,128)(2,1)S(1)} %bitcast.283), channel_id=1, replica_groups=mesh['grp'=32,'tp'=8] {'tp'}, dimensions={0}, use_global_device_ids=true | all-gather | bytes 18432 | tf_op jit(solution)/shard_map/all_gather | solution.py:145
  244.7 99.7 %all-reduce.8.cloned.1.call-done = (f32[512,2,2048]{2,1,0:T(2,128)}, f32[512,2,32]{2,1,0:T(2,128)}, f32[512,2,32]{2,1,0:T(2,128)}) async-done(((f32[512,2,2048]{2,1,0:T(2,128)}, f32[512,2,32]{2,1,0:T(2,128)}, f32[512,2,32]{2,1,0:T(2,128)}), (f32[512,2,2048]{2,1,0:T(2,128)}, f32[512,2,32]{2,1,0:T(2,128)}, f32[512,2,32]{2,1,0:T(2,128)})) %all-reduce.8.cloned.1.call-update) | async-done | bytes 8650768
  346.6 26.0 %all_gather.28 = bf16[8,16,4,8]{1,3,2,0:T(8,128)(2,1)S(1)} all-gather(bf16[1,16,4,8]{1,3,2,0:T(8,128)(2,1)S(1)} %fusion.49), channel_id=1, replica_groups=mesh['grp'=32,'tp'=8] {'tp'}, dimensions={0}, use_global_device_ids=true | all-gather | bytes 9216 | tf_op jit(solution)/shard_map/all_gather | solution.py:15
  376.1 26.8 %all-gather = bf16[128,4,8,64]{3,2,1,0:T(8,128)(2,1)S(1)} all-gather(bf16[16,4,8,64]{3,2,1,0:T(8,128)(2,1)S(1)} %fusion.9), channel_id=2, replica_groups=mesh['grp'=32,'tp'=8] {'tp'}, dimensions={0}, use_global_device_ids=true | all-gather | bytes 589824 | tf_op jit(solution)/shard_map/all_gather | solution.py:15
  402.9 24.6 %all_gather.27 = bf16[8,16,4,8]{1,3,2,0:T(8,128)(2,1)S(1)} all-gather(bf16[1,16,4,8]{1,3,2,0:T(8,128)(2,1)S(1)} %fusion.56), channel_id=1, replica_groups=mesh['grp'=32,'tp'=8] {'tp'}, dimensions={0}, use_global_device_ids=true | all-gather | bytes 9216 | tf_op jit(solution)/shard_map/all_gather | solution.py:15
  427.5 3.9 while.19
  432.9 35.4 %reduce-scatter.2.cloned.1.call-done = bf16[16,256]{1,0:T(8,128)(2,1)} async-done(((bf16[16,2048]{1,0:T(8,128)(2,1)}), bf16[16,256]{1,0:T(8,128)(2,1)}) %reduce-scatter.2.cloned.1.call-update) | async-done | bytes 8208 | tf_op jit(solution)/shard_map/reduce_scatter | solution.py:213
  (199 shorter events, 52.2 us)
Async XLA Ops:
  7.2 424.8 %copy-start = (bf16[256,2048]{1,0:T(8,128)(2,1)S(1)}, bf16[256,2048]{1,0:T(8,128)(2,1)}, u32[]{:S(2)}) copy-start(bf16[256,2048]{1,0:T(8,128)(2,1)} %param.19) | copy-start | bytes 3145732
  7.2 103.0 %all-gather.4.cloned.1.call-start = ((), (), s32[]{:S(2)}) async-start(), calls=%async_computation.1 | async-start | bytes 2162688 | tf_op jit(solution)/shard_map/all_gather | solution.py:147
  7.2 102.9 %copy-start.18 = (f32[32]{0:T(128)}, f32[32]{0:T(128)S(1)}, u32[]{:S(2)}) copy-start(f32[32]{0:T(128)S(1)} %multiply_exponential_fusion) | copy-start | bytes 388
  13.7 1.6 copy-start.21
  16.1 94.1 %copy-start.13 = (f32[16]{0:T(128)}, f32[16]{0:T(128)S(1)}, u32[]{:S(2)}) copy-start(f32[16]{0:T(128)S(1)} %add_convert_fusion.2) | copy-start | bytes 196
  46.7 297.8 %all-reduce.8.cloned.1.call-start = ((), (), s32[]{:S(2)}) async-start(), calls=%async_computation.3 | async-start | bytes 18874368
  108.1 16.5 %copy-start.17 = (pred[128]{0:T(512)(128)(4,1)}, pred[128]{0:T(512)(128)(4,1)S(1)}, u32[]{:S(2)}) copy-start(pred[128]{0:T(512)(128)(4,1)S(1)} %iota_compare_fusion.1) | copy-start | bytes 388
  108.8 16.2 %copy-start.15 = (pred[128]{0:T(512)(128)(4,1)}, pred[128]{0:T(512)(128)(4,1)S(1)}, u32[]{:S(2)}) copy-start(pred[128]{0:T(512)(128)(4,1)S(1)} %iota_compare_fusion) | copy-start | bytes 388
  110.0 9.8 %copy-start.12 = (pred[64]{0:T(512)(128)(4,1)}, pred[64]{0:T(512)(128)(4,1)S(1)}, u32[]{:S(2)}) copy-start(pred[64]{0:T(512)(128)(4,1)S(1)} %get-tuple-element.351) | copy-start | bytes 196
  110.0 14.6 %copy-start.11 = (pred[64]{0:T(512)(128)(4,1)}, pred[64]{0:T(512)(128)(4,1)S(1)}, u32[]{:S(2)}) copy-start(pred[64]{0:T(512)(128)(4,1)S(1)} %get-tuple-element.350) | copy-start | bytes 196
  110.2 11.0 %copy-start.1 = (bf16[512,2048]{1,0:T(8,128)(2,1)S(1)}, bf16[512,2048]{1,0:T(8,128)(2,1)}, u32[]{:S(2)}) copy-start(bf16[512,2048]{1,0:T(8,128)(2,1)} %all-gather.4.cloned.1.call-done) | copy-start | bytes 6291460
  119.8 1.2 copy-start.8
  127.2 6.3 %copy-start.16 = (pred[128]{0:T(512)(128)(4,1)S(1)}, pred[128]{0:T(512)(128)(4,1)}, u32[]{:S(2)}) copy-start(pred[128]{0:T(512)(128)(4,1)} %copy-done.15) | copy-start | bytes 388
  154.9 35.3 %copy-start.3 = (f32[512,2,32]{2,1,0:T(2,128)}, f32[512,2,32]{2,1,0:T(2,128)S(1)}, u32[]{:S(2)}) copy-start(f32[512,2,32]{2,1,0:T(2,128)S(1)} %scatter_fusion.5) | copy-start | bytes 393220
  161.5 28.7 %copy-start.4 = (f32[512,2,32]{2,1,0:T(2,128)}, f32[512,2,32]{2,1,0:T(2,128)S(1)}, u32[]{:S(2)}) copy-start(f32[512,2,32]{2,1,0:T(2,128)S(1)} %scatter_fusion.3) | copy-start | bytes 393220
  213.0 1.3 copy-start.5
  213.0 1.8 copy-start.20
  213.0 4.2 copy-start.7
  213.0 4.2 copy-start.22
  213.0 5.3 %copy-start.14 = (f32[16]{0:T(128)S(1)}, f32[16]{0:T(128)}, u32[]{:S(2)}) copy-start(f32[16]{0:T(128)} %copy-done.13) | copy-start | bytes 196
  213.0 5.3 %copy-start.19 = (f32[32]{0:T(128)S(1)}, f32[32]{0:T(128)}, u32[]{:S(2)}) copy-start(f32[32]{0:T(128)} %copy-done.18) | copy-start | bytes 388
  213.0 30.3 %copy-start.23 = (u32[256]{0:T(256)S(1)}, u32[256]{0:T(256)}, u32[]{:S(2)}) copy-start(u32[256]{0:T(256)} %constant.274) | copy-start | bytes 3076
  213.1 255.2 %reduce-scatter.2.cloned.1.call-start = ((), (), s32[]{:S(2)}) async-start(), calls=%async_computation.2 | async-start | bytes 73728 | tf_op jit(solution)/shard_map/reduce_scatter | solution.py:213
  218.5 214.3 %copy-start.10 = (bf16[16,64]{1,0:T(8,128)(2,1)}, bf16[16,64]{1,0:T(8,128)(2,1)S(1)}, u32[]{:S(2)}) copy-start(bf16[16,64]{1,0:T(8,128)(2,1)S(1)} %fusion.71) | copy-start | bytes 6148
  (3 other events, 2.4 us)
Sparse Core Ops, SparseCore 0:
  46.8 46.4 all-gather.3
  213.2 131.2 all-reduce.7
  433.0 35.2 reduce-scatter.1
where the time goes:
time: 478 us; the launch traced here: 476 us
  other arithmetic  137 us (29%)
  waiting for transfers between devices  135 us (28%)
  blocking collectives  132 us (28%)
  local copies, waits for them, and re-layouts  44.5 us (9%)
  between operations  15.1 us (3%)
  matrix products  11.6 us (2%)
    unnamed x4, waiting for transfers between devices  99.7 us
    all_gather x3, blocking collectives, combined_all(): lax.all_gather(part.astype(kind), axis)  77.3 us
    scatter-add x2, other arithmetic, on_device(): sum_rows.at[picked, level_slot]  43.9 us
    reduce_sum x2, other arithmetic, on_device(): filled = jnp.arange(per_tenant) < jnp.sum(member.astype(jnp.int32))  42.6 us
    reduce_scatter x1, waiting for transfers between devices, on_device(): lax.psum_scatter(projected.astype(jnp.bfloat16), 'tp', scatter_dimension=...  35.4 us
    all_gather x1, blocking collectives, on_device(): lax.all_gather(query_rot, 'tp', axis=1, tiled=True)  30.2 us
    all_gather x1, blocking collectives, on_device(): lax.all_gather(new_keyval, 'tp', axis=1, tiled=True)  24.5 us
    scatter-add x2, other arithmetic, on_device(): total_rows.at[picked, level_slot]  13.4 us
  transfers between devices with their start and end apart: 3, of which 2 were waited for; matrix products, arithmetic and copies ran while one was open for 14% of the time, Pallas kernels for 0%

commit v1 on v0

--- a/solution.py
+++ b/solution.py
@@ -8,6 +8,11 @@
 KV_HEADS = 4
 HEAD_DIM = 64
 TENANTS = 4
+
+
+def gather_by_exchange(x, axis, dim):
+    copies = jnp.concatenate([x] * lax.axis_size(axis), axis=dim)
+    return lax.all_to_all(copies, axis, dim, dim, tiled=True)
 
 
 def combined_all(x, axis, combine):
@@ -141,7 +146,7 @@
         .astype(jnp.bfloat16)
     )
     query_all, keyval_all = (
-        lax.all_gather(query_rot, "tp", axis=1, tiled=True),
+        gather_by_exchange(query_rot, "tp", 1),
         lax.all_gather(new_keyval, "tp", axis=1, tiled=True),
     )
     everyone = lax.all_gather(query_all, "grp", axis=0, tiled=True)

time: 478 us -> 464 us (0.971)
  blocking collectives: 132 us -> 118 us
    all_gather x1 -> x0, blocking collectives: 30.2 us -> none  [on_device(): lax.all_gather(query_rot, 'tp', axis=1, tiled=True)]
    all_to_all x0 -> x1, blocking collectives: none -> 16.6 us  [gather_by_exchange(): return lax.all_to_all(copies, axis, dim, dim, tiled=True)]
  transfers between devices with their start and end apart: 3 -> 3, of which waited for: 2 -> 2; matrix products, arithmetic and copies ran while one was open for 14% -> 15% of each run, Pallas kernels for 0% -> 0%
where the time goes in v1:
time: 464 us; the launch traced here: 462 us
  other arithmetic  138 us (30%)
  waiting for transfers between devices  132 us (28%)
  blocking collectives  118 us (25%)
  local copies, waits for them, and re-layouts  45.8 us (10%)
  between operations  15.1 us (3%)
  matrix products  11.5 us (2%)
    unnamed x4, waiting for transfers between devices  96.7 us
    all_gather x3, blocking collectives, combined_all(): lax.all_gather(part.astype(kind), axis)  77.3 us
    scatter-add x2, other arithmetic, on_device(): sum_rows.at[picked, level_slot]  43.9 us
    reduce_sum x2, other arithmetic, on_device(): filled = jnp.arange(per_tenant) < jnp.sum(member.astype(jnp.int32))  42.8 us
    reduce_scatter x1, waiting for transfers between devices, on_device(): lax.psum_scatter(projected.astype(jnp.bfloat16), 'tp', scatter_dimension=...  35.4 us
    all_gather x1, blocking collectives, on_device(): lax.all_gather(new_keyval, 'tp', axis=1, tiled=True)  24.5 us
    all_to_all x1, blocking collectives, gather_by_exchange(): return lax.all_to_all(copies, axis, dim, dim, tiled=True)  16.6 us
    scatter-add x2, other arithmetic, on_device(): total_rows.at[picked, level_slot]  13.4 us
  transfers between devices with their start and end apart: 3, of which 2 were waited for; matrix products, arithmetic and copies ran while one was open for 15% of the time, Pallas kernels for 0%

profile of v1, /device:TPU:10, one launch (start us, length us, event | category | flops | bytes accessed | tf_op | source)
XLA Modules:
  0.0 461.5 jit_solution(16420659284515333162)
XLA Ops:
  16.5 16.6 %all_to_all.9 = bf16[16,8,256]{2,0,1:T(8,128)(2,1)S(1)} all-to-all(bf16[16,8,256]{2,0,1:T(8,128)(2,1)S(1)} %concatenate.28), channel_id=1, replica_groups=mesh['grp'=32,'tp'=8] {'tp'}, dimensions={1} | all-to-all | bytes 131072 | tf_op jit(solution)/shard_map/all_to_all | solution.py:15
  37.4 2.1 fusion.87
  39.5 2.1 fusion.88
  41.5 2.1 fusion.89
  43.6 41.5 %convert_reduce_fusion = (s32[]{:T(128)}, pred[512]{0:T(512)(128)(4,1)S(1)}, s32[512]{0:T(512)S(1)}) fusion(s32[512]{0:T(512)} %param.24, s32[]{:T(128)S(6)} %add.231, pred[]{:T(512)S(6)} %lt.150, s32[]{:T(128)} %bitcast.67, s32[]{:T(128)} %bitcast.66, s32[]{:T(128)} %bitcast.65, s32[]{:T(128)} %bitcast.64, s32[]{:T(128)} %bitcast.63, s32[]{:T(128)} %bitcast.62, ...), kind=kLoop, calls=%fused_computation.153 | loop fusion | flops 68607 | bytes 4873 | tf_op jit(solution)/shard_map/reduce_sum | solution.py:165
  86.5 3.8 top_k.17
  90.3 3.8 top_k.24
  98.0 4.3 gather_fusion.3
  104.2 2.0 copy.77
  117.7 2.1 fusion.16
  123.2 6.8 %scatter_fusion.4 = f32[512,2,32]{2,1,0:T(2,128)S(1)} fusion(f32[512,2,32]{2,1,0:T(2,128)S(1)} %broadcast.256.clone.1, s32[128]{0:T(128)S(1)} %fusion.77, f32[128,32]{1,0:T(8,128)S(1)} %copy.98), kind=kCustom, calls=%fused_computation.9 | custom fusion | flops 4096 | bytes 50176 | tf_op jit(solution)/shard_map/scatter-add | solution.py:186
  130.2 6.6 %scatter_fusion.2 = f32[512,2,32]{2,1,0:T(2,128)S(1)} fusion(f32[512,2,32]{2,1,0:T(2,128)S(1)} %broadcast.256.clone, s32[128]{0:T(128)S(1)} %fusion.77, f32[128,32]{1,0:T(8,128)S(1)} %copy.86), kind=kCustom, calls=%fused_computation.7 | custom fusion | flops 4096 | bytes 50176 | tf_op jit(solution)/shard_map/scatter-add | solution.py:183
  136.8 6.6 %scatter_fusion.5 = f32[512,2,32]{2,1,0:T(2,128)S(1)} fusion(f32[512,2,32]{2,1,0:T(2,128)S(1)} %scatter_fusion.4, s32[128]{0:T(128)S(1)} %fusion.78, f32[128,32]{1,0:T(8,128)S(1)} %copy.99), kind=kCustom, calls=%fused_computation.10 | custom fusion | flops 4096 | bytes 50176 | tf_op jit(solution)/shard_map/scatter-add | solution.py:186
  143.4 6.6 %scatter_fusion.3 = f32[512,2,32]{2,1,0:T(2,128)S(1)} fusion(f32[512,2,32]{2,1,0:T(2,128)S(1)} %scatter_fusion.2, s32[128]{0:T(128)S(1)} %fusion.78, f32[128,32]{1,0:T(8,128)S(1)} %copy.87), kind=kCustom, calls=%fused_computation.8 | custom fusion | flops 4096 | bytes 50176 | tf_op jit(solution)/shard_map/scatter-add | solution.py:183
  150.0 7.5 %broadcast_in_dim.180 = f32[512,2,2048]{2,1,0:T(2,128)} broadcast(f32[]{:T(128)} %constant.85.clone.1), dimensions={} | broadcast | bytes 8388612 | tf_op jit(solution)/shard_map/broadcast_in_dim | solution.py:174
  157.5 21.2 %scatter_fusion = f32[512,2,2048]{2,1,0:T(2,128)} fusion(f32[512,2,2048]{2,1,0:T(2,128)} %broadcast_in_dim.180, s32[128]{0:T(128)S(1)} %fusion.77, f32[128,2048]{1,0:T(8,128)S(1)} %broadcast_select_fusion.1), kind=kCustom, calls=%fused_computation.5 | custom fusion | flops 262144 | bytes 3146752 | tf_op jit(solution)/shard_map/scatter-add | solution.py:180
  178.7 22.7 %scatter_fusion.1 = f32[512,2,2048]{2,1,0:T(2,128)} fusion(f32[512,2,2048]{2,1,0:T(2,128)} %scatter_fusion, s32[128]{0:T(128)S(1)} %fusion.78, f32[128,2048]{1,0:T(8,128)} %broadcast_select_fusion), kind=kCustom, calls=%fused_computation.6 | custom fusion | flops 262144 | bytes 3146752 | tf_op jit(solution)/shard_map/scatter-add | solution.py:180
  206.0 24.5 %all-gather.1 = bf16[8,64,16]{1,2,0:T(8,128)(2,1)S(1)} all-gather(bf16[1,64,16]{1,2,0:T(8,128)(2,1)S(1)} %bitcast.287), channel_id=1, replica_groups=mesh['grp'=32,'tp'=8] {'tp'}, dimensions={0}, use_global_device_ids=true | all-gather | bytes 18432 | tf_op jit(solution)/shard_map/all_gather | solution.py:150
  233.3 96.6 %all-reduce.8.cloned.1.call-done = (f32[512,2,2048]{2,1,0:T(2,128)}, f32[512,2,32]{2,1,0:T(2,128)}, f32[512,2,32]{2,1,0:T(2,128)}) async-done(((f32[512,2,2048]{2,1,0:T(2,128)}, f32[512,2,32]{2,1,0:T(2,128)}, f32[512,2,32]{2,1,0:T(2,128)}), (f32[512,2,2048]{2,1,0:T(2,128)}, f32[512,2,32]{2,1,0:T(2,128)}, f32[512,2,32]{2,1,0:T(2,128)})) %all-reduce.8.cloned.1.call-update) | async-done | bytes 8650768
  332.0 26.0 %all_gather.24 = bf16[8,16,4,8]{1,3,2,0:T(8,128)(2,1)S(1)} all-gather(bf16[1,16,4,8]{1,3,2,0:T(8,128)(2,1)S(1)} %fusion.49), channel_id=1, replica_groups=mesh['grp'=32,'tp'=8] {'tp'}, dimensions={0}, use_global_device_ids=true | all-gather | bytes 9216 | tf_op jit(solution)/shard_map/all_gather | solution.py:20
  361.5 26.8 %all-gather = bf16[128,4,8,64]{3,2,1,0:T(8,128)(2,1)S(1)} all-gather(bf16[16,4,8,64]{3,2,1,0:T(8,128)(2,1)S(1)} %fusion.9), channel_id=2, replica_groups=mesh['grp'=32,'tp'=8] {'tp'}, dimensions={0}, use_global_device_ids=true | all-gather | bytes 589824 | tf_op jit(solution)/shard_map/all_gather | solution.py:20
  388.3 24.6 %all_gather.23 = bf16[8,16,4,8]{1,3,2,0:T(8,128)(2,1)S(1)} all-gather(bf16[1,16,4,8]{1,3,2,0:T(8,128)(2,1)S(1)} %fusion.56), channel_id=1, replica_groups=mesh['grp'=32,'tp'=8] {'tp'}, dimensions={0}, use_global_device_ids=true | all-gather | bytes 9216 | tf_op jit(solution)/shard_map/all_gather | solution.py:20
  413.0 3.9 while.19
  418.3 35.4 %reduce-scatter.2.cloned.1.call-done = bf16[16,256]{1,0:T(8,128)(2,1)} async-done(((bf16[16,2048]{1,0:T(8,128)(2,1)}), bf16[16,256]{1,0:T(8,128)(2,1)}) %reduce-scatter.2.cloned.1.call-update) | async-done | bytes 8208 | tf_op jit(solution)/shard_map/reduce_scatter | solution.py:218
  (198 shorter events, 54.1 us)
Async XLA Ops:
  7.2 410.3 %copy-start = (bf16[256,2048]{1,0:T(8,128)(2,1)S(1)}, bf16[256,2048]{1,0:T(8,128)(2,1)}, u32[]{:S(2)}) copy-start(bf16[256,2048]{1,0:T(8,128)(2,1)} %param.19) | copy-start | bytes 3145732
  7.2 90.8 %all-gather.4.cloned.1.call-start = ((), (), s32[]{:S(2)}) async-start(), calls=%async_computation.2 | async-start | bytes 2162688 | tf_op jit(solution)/shard_map/all_gather | solution.py:152
  7.2 27.5 %copy-start.16 = (f32[32]{0:T(128)}, f32[32]{0:T(128)S(1)}, u32[]{:S(2)}) copy-start(f32[32]{0:T(128)S(1)} %multiply_exponential_fusion) | copy-start | bytes 388
  13.7 1.6 copy-start.19
  16.1 18.7 %copy-start.12 = (f32[16]{0:T(128)}, f32[16]{0:T(128)S(1)}, u32[]{:S(2)}) copy-start(f32[16]{0:T(128)S(1)} %add_convert_fusion.2) | copy-start | bytes 196
  33.8 296.1 %all-reduce.8.cloned.1.call-start = ((), (), s32[]{:S(2)}) async-start(), calls=%async_computation.4 | async-start | bytes 18874368
  96.0 16.5 %copy-start.15 = (pred[128]{0:T(512)(128)(4,1)}, pred[128]{0:T(512)(128)(4,1)S(1)}, u32[]{:S(2)}) copy-start(pred[128]{0:T(512)(128)(4,1)S(1)} %iota_compare_fusion.1) | copy-start | bytes 388
  96.6 16.1 %copy-start.14 = (pred[128]{0:T(512)(128)(4,1)}, pred[128]{0:T(512)(128)(4,1)S(1)}, u32[]{:S(2)}) copy-start(pred[128]{0:T(512)(128)(4,1)S(1)} %iota_compare_fusion) | copy-start | bytes 388
  97.9 9.8 %copy-start.11 = (pred[64]{0:T(512)(128)(4,1)}, pred[64]{0:T(512)(128)(4,1)S(1)}, u32[]{:S(2)}) copy-start(pred[64]{0:T(512)(128)(4,1)S(1)} %get-tuple-element.351) | copy-start | bytes 196
  97.9 14.6 %copy-start.10 = (pred[64]{0:T(512)(128)(4,1)}, pred[64]{0:T(512)(128)(4,1)S(1)}, u32[]{:S(2)}) copy-start(pred[64]{0:T(512)(128)(4,1)S(1)} %get-tuple-element.350) | copy-start | bytes 196
  98.0 11.0 %copy-start.1 = (bf16[512,2048]{1,0:T(8,128)(2,1)S(1)}, bf16[512,2048]{1,0:T(8,128)(2,1)}, u32[]{:S(2)}) copy-start(bf16[512,2048]{1,0:T(8,128)(2,1)} %all-gather.4.cloned.1.call-done) | copy-start | bytes 6291460
  107.6 1.0 copy-start.2
  107.6 1.2 copy-start.7
  143.4 35.3 %copy-start.3 = (f32[512,2,32]{2,1,0:T(2,128)}, f32[512,2,32]{2,1,0:T(2,128)S(1)}, u32[]{:S(2)}) copy-start(f32[512,2,32]{2,1,0:T(2,128)S(1)} %scatter_fusion.5) | copy-start | bytes 393220
  150.0 28.7 %copy-start.4 = (f32[512,2,32]{2,1,0:T(2,128)}, f32[512,2,32]{2,1,0:T(2,128)S(1)}, u32[]{:S(2)}) copy-start(f32[512,2,32]{2,1,0:T(2,128)S(1)} %scatter_fusion.3) | copy-start | bytes 393220
  201.4 1.2 copy-start.5
  201.4 3.2 copy-start.6
  201.4 3.2 copy-start.20
  201.4 4.4 copy-start.13
  201.4 4.4 copy-start.17
  201.4 29.3 %copy-start.21 = (u32[256]{0:T(256)S(1)}, u32[256]{0:T(256)}, u32[]{:S(2)}) copy-start(u32[256]{0:T(256)} %constant.274) | copy-start | bytes 3076
  201.4 30.6 %copy-start.18 = (s32[16]{0:T(128)S(1)}, s32[16]{0:T(128)}, u32[]{:S(2)}) copy-start(s32[16]{0:T(128)} %param.25) | copy-start | bytes 196
  201.5 252.2 %reduce-scatter.2.cloned.1.call-start = ((), (), s32[]{:S(2)}) async-start(), calls=%async_computation.3 | async-start | bytes 73728 | tf_op jit(solution)/shard_map/reduce_scatter | solution.py:218
  206.0 207.0 %copy-start.9 = (bf16[16,64]{1,0:T(8,128)(2,1)}, bf16[16,64]{1,0:T(8,128)(2,1)S(1)}, u32[]{:S(2)}) copy-start(bf16[16,64]{1,0:T(8,128)(2,1)S(1)} %fusion.71) | copy-start | bytes 6148
  (1 other events, 0.6 us)
Sparse Core Ops, SparseCore 0:
  33.9 43.4 all-gather.3
  201.6 128.2 all-reduce.7
  418.5 35.2 reduce-scatter.1
